TPU v7x, 32 devices: a whole 2x2x4 slice. The times are simulated.
32 devices in a mesh: vol: 8 (over z, x), mem: 4 (over y, core).
Axes of the slice: x: 2, y: 2, z: 4, core: 2. Of those that a mesh axis runs over, the one named last changes fastest.
Arguments:
- potential: float32 [32, 256, 1024], P('vol', 'mem'), may hold values from -6 to 6
- conductivity: float32 [32, 256, 1024], P('vol', 'mem'), may hold values from 0.1 to 4
- ion_states: float32 [40, 524288], P(None, ('vol', 'mem')), may hold values from 0 to 1
- rate_scale: float32 [2, 40], replicated, may hold values from 0.05 to 2
- rate_slope: float32 [2, 40], replicated, may hold values from -1 to 1
- type_cond: float32 [3, 40], replicated, may hold values from 0.005 to 0.05
- reversal: float32 [40], replicated, may hold values from -2 to 2
- facet_counts: int32 [2048], P(('vol', 'mem')), may hold values from 0 to 256, as said below
- intra_voxel: int32 [524288], P(('vol', 'mem')), may hold values from 0 to 262143, as said below
- extra_voxel: int32 [524288], P(('vol', 'mem')), may hold values from 0 to 262143, as said below
- cell_type: int32 [2048], P(('vol', 'mem')), may hold values from 0 to 2
- gap_partner: int32 [2048, 8], P(('vol', 'mem')), may hold values from 0 to 2047, as said below
- gap_cond: float32 [2048, 8], P(('vol', 'mem')), may hold values from 0.2 to 2
Outputs:
- potential_next: float32 [32, 256, 1024], P('vol', 'mem')
- states_next: float32 [40, 524288], P(None, ('vol', 'mem'))
- membrane_current: float32 [524288], P(('vol', 'mem'))
Inputs may be any that keep to these rules, and one draw needn't show every extreme that they name: `facet_counts`: within each brick's 64 cell slots, the cells with a positive count come first; a used cell has 64 to 256 facets; some brick has all its cells used and some cell uses all 256 slots. `intra_voxel`: local index x * 64 * 1024 + y * 1024 + z within the brick that holds the facet; the facets of the cell in slot s of its brick lie in local indices s * R to s * R + R - 1, with R = 4096. `extra_voxel`: local index x * 64 * 1024 + y * 1024 + z within the brick that holds the facet; the facets of the cell in slot s of its brick lie in local indices s * R to s * R + R - 1, with R = 4096. `gap_partner`: each partner is a cell with a positive count, in a brick whose first brick index differs from its own cell's by at most one.
All inputs are finite; a program needn't handle non-finite values.
Results may differ from a plain program's by a relative error of at most 0.0003.
Values sent between devices are 32-bit elements; how exact they have to be, the bound alone decides.
A program may use at most 64 MiB of HBM per device.

v0:
```python
import functools

import jax
import jax.numpy as jnp
from jax import lax
from jax.experimental import pallas as pl
from jax.experimental.pallas import tpu as pltpu
from jax.sharding import PartitionSpec as P

ITERS = 4
CHUNKS = 4

mass_coef = 1.0
time_step = 0.5
low_eig = 0.2
high_eig = 1.8

MESH = pl.DeviceIdType.MESH
F32 = jnp.float32
BF16 = jnp.bfloat16


def sweep_weights():
    theta = 0.5 * (high_eig + low_eig)
    delta = 0.5 * (high_eig - low_eig)
    sigma_one = theta / delta
    rho = 1.0 / sigma_one
    pairs = [(0.0, 1.0 / theta)]
    for _ in range(ITERS - 1):
        rho_next = 1.0 / (2.0 * sigma_one - rho)
        pairs.append((rho_next * rho, 2.0 * rho_next / delta))
        rho = rho_next
    return pairs


def split2(x):
    hi = x.astype(BF16)
    lo = (x - hi.astype(F32)).astype(BF16)
    return hi, lo


def kernel(
    n_vol, n_mem, ntypes,
    *refs,
):
    count = 13
    given, outs, held = refs[:count], refs[count:count + 3], refs[count + 3:2 * count + 3]
    body(n_vol, n_mem, ntypes, given, *held, *outs, *refs[2 * count + 3:])


def body(
    n_vol, n_mem, ntypes, given,
    pot, cond, states, rate_scale, rate_slope, type_cond, reversal, counts, kinds, intra, extra, partner, gcond,
    out_pot, out_states, out_cur,
    sl,
    X, C, K, R, U, HX, YS, YR, LT, PB, VOLT, CVS, CV,
    sx_send, sx_recv, sy_send, sy_recv, sc_send, sc_recv,
):
    held = (pot, cond, states, rate_scale, rate_slope, type_cond, reversal, counts, kinds, intra, extra, partner, gcond)
    loads = [pltpu.make_async_copy(src, dst, sl.at[i]) for i, (src, dst) in enumerate(zip(given, held))]
    for i in (1, 0, 9, 10, 7, 8, 3, 4, 5, 6, 2, 11, 12):
        loads[i].start()
    CX, CY, CZ = pot.shape
    nstates, facets = states.shape
    cells = counts.shape[0]
    fpc = facets // cells
    groups, _, gf = intra.shape
    gcells = gf // fpc
    ybs = CY // 8
    zts = CZ // 128
    crow = CY // CHUNKS
    me_v = lax.axis_index("vol")
    me_m = lax.axis_index("mem")
    has = ((me_v > 0, me_v < n_vol - 1), (me_m > 0, me_m < n_mem - 1))

    peers = []
    for dv in (-1, 0, 1):
        for dm in range(n_mem):
            if dv == 0 and dm == 0:
                continue
            other_m = lax.rem(me_m + dm, n_mem)
            ok = None if dv == 0 else has[0][0 if dv < 0 else 1]
            peers.append((dv, dm, other_m, ok))

    def guarded(ok, fn):
        if ok is None:
            fn()
        else:
            pl.when(ok)(fn)

    barrier = pltpu.get_barrier_semaphore()
    for dv, dm, other_m, ok in peers:
        def greet(dv=dv, other_m=other_m):
            pl.semaphore_signal(barrier, inc=1, device_id=(me_v + dv, other_m), device_id_type=MESH)
        guarded(ok, greet)
    columns = 1 + has[0][0].astype(jnp.int32) + has[0][1].astype(jnp.int32)
    pl.semaphore_wait(barrier, columns * n_mem - 1)

    def x_copy(e, side, ch, plane_ref):
        rows = pl.ds(ch * crow, crow)
        return pltpu.make_async_remote_copy(
            src_ref=plane_ref,
            dst_ref=HX.at[e, 1 - side, rows],
            send_sem=sx_send.at[e, side, ch],
            recv_sem=sx_recv.at[e, 1 - side, ch],
            device_id=(me_v + (1 if side else -1), me_m),
            device_id_type=MESH,
        )

    def y_copy(e, side):
        return pltpu.make_async_remote_copy(
            src_ref=YS.at[e, side],
            dst_ref=YR.at[e, 1 - side],
            send_sem=sy_send.at[e, side],
            recv_sem=sy_recv.at[e, 1 - side],
            device_id=(me_v, me_m + (1 if side else -1)),
            device_id_type=MESH,
        )

    def face_of(e, side, ch):
        plane = CX - 1 if side else 0
        if e == 0:
            return cond.at[plane, pl.ds(ch * crow, crow)]
        if e == 1:
            return pot.at[plane, pl.ds(ch * crow, crow)]
        return X.at[e - 1, plane, pl.ds(8 + ch * crow, crow)]

    def send_x(e, ch):
        for side in (0, 1):
            guarded(has[0][side], lambda side=side: x_copy(e, side, ch, face_of(e, side, ch)).start())

    def wait_x(e, ch):
        for side in (0, 1):
            def w(side=side):
                pltpu.make_async_remote_copy(
                    src_ref=HX.at[e, side, pl.ds(ch * crow, crow)],
                    dst_ref=HX.at[e, side, pl.ds(ch * crow, crow)],
                    send_sem=sx_send.at[e, side, ch],
                    recv_sem=sx_recv.at[e, side, ch],
                    device_id=(me_v + (1 if side else -1), me_m),
                    device_id_type=MESH,
                ).wait_recv()
            guarded(has[0][side], w)

    def send_y(e):
        for side in (0, 1):
            guarded(has[1][side], lambda side=side: y_copy(e, side).start())

    def wait_y(e):
        for side in (0, 1):
            def w(side=side):
                pltpu.make_async_remote_copy(
                    src_ref=YS.at[e, side],
                    dst_ref=YR.at[e, side],
                    send_sem=sy_send.at[e, side],
                    recv_sem=sy_recv.at[e, side],
                    device_id=(me_v, me_m + (1 if side else -1)),
                    device_id_type=MESH,
                ).wait_recv()
            guarded(has[1][side], w)

    for e in (0, 1):
        ref = (cond, pot)[e]
        loads[1 - e].wait()
        for ch in range(CHUNKS):
            send_x(e, ch)
        for p in range(CX):
            YS[e, 0, p:p + 1, :] = ref[p, 0:1, :]
            YS[e, 1, p:p + 1, :] = ref[p, CY - 1:CY, :]
        send_y(e)

    for i in range(2, len(loads)):
        loads[i].wait()

    for side in (0, 1):
        @pl.when(jnp.logical_not(has[0][side]))
        def _(side=side):
            def zero(i, c):
                for e in range(ITERS + 1):
                    HX[e, side, pl.ds(pl.multiple_of(i * 8, 8), 8), :] = jnp.zeros((8, CZ), F32)
                return c
            lax.fori_loop(0, ybs, zero, 0)
            for dm in range(n_mem):
                CV[(2 if side else 0) * n_mem + dm] = jnp.zeros((8, 128), F32)

        @pl.when(jnp.logical_not(has[1][side]))
        def _(side=side):
            for e in range(ITERS + 1):
                YR[e, side] = jnp.zeros((8, CZ), F32)

    eye = lax.broadcasted_iota(jnp.int32, (nstates, nstates), 0) == lax.broadcasted_iota(
        jnp.int32, (nstates, nstates), 1
    )
    columns = [rate_scale[0:1, :], rate_slope[0:1, :], rate_scale[1:2, :], rate_slope[1:2, :]]
    columns += [reversal[...]] + [type_cond[k:k + 1, :] for k in range(ntypes)]
    for k, col in enumerate(columns):
        spread = jnp.where(eye, jnp.broadcast_to(col, (nstates, nstates)), 0.0)
        PB[k] = jnp.broadcast_to(jnp.sum(spread, axis=1, keepdims=True), (nstates, 128))

    lane1 = lax.broadcasted_iota(jnp.int32, (1, 128), 1)
    slot_k = lax.broadcasted_iota(jnp.int32, (1, fpc), 1)

    def gather(g, acc):
        gx, gy = g // ybs, g % ybs
        tile = pot[gx, pl.ds(pl.multiple_of(gy * 8, 8), 8), :]
        block = jnp.concatenate([tile[:, z * 128:(z + 1) * 128] for z in range(zts)], axis=0)
        hi, lo = split2(block)
        lhs = jnp.concatenate([hi, lo], axis=0)
        picked = []
        for i, ref in enumerate((intra, extra)):
            idx = ref[g]
            lane = idx & 127
            row = ((idx >> 7) & (zts - 1)) * 8 + ((idx // CZ) & 7)
            hot = lax.broadcasted_iota(jnp.int32, (128, gf), 0) == lane
            table = jnp.where(hot, 1.0, 0.0).astype(BF16)
            LT[g, i] = table
            got = jnp.dot(lhs, table, preferred_element_type=F32)
            half = got.shape[0] // 2
            got = got[:half] + got[half:]
            mask = lax.broadcasted_iota(jnp.int32, (8 * zts, gf), 0) == row
            picked.append(jnp.sum(jnp.where(mask, got, 0.0), axis=0, keepdims=True))
        volt = picked[0] - picked[1]
        VOLT[g] = volt
        for q in range(gcells):
            c = g * gcells + q
            cnt = counts[c]
            part = jnp.where(slot_k < cnt, volt[:, q * fpc:(q + 1) * fpc], 0.0)
            total = jnp.sum(part, axis=1, keepdims=True)
            div = jnp.maximum(jnp.full((1, 128), cnt, jnp.int32), 1).astype(F32)
            acc = jnp.where(lane1 == c, total / div, acc)
        return acc

    cell_volt = lax.fori_loop(0, groups, gather, jnp.zeros((1, 128), F32))
    CVS[...] = jnp.broadcast_to(cell_volt, (8, 128))
    CV[n_mem + me_m] = jnp.broadcast_to(cell_volt, (8, 128))

    def cv_copy(dv, dm, other_m):
        return pltpu.make_async_remote_copy(
            src_ref=CVS,
            dst_ref=CV.at[(1 - dv) * n_mem + me_m],
            send_sem=sc_send.at[(dv + 1) * n_mem + dm],
            recv_sem=sc_recv.at[(1 - dv) * n_mem + me_m],
            device_id=(me_v + dv, other_m),
            device_id_type=MESH,
        )

    def cv_wait(dv, dm, other_m):
        pltpu.make_async_remote_copy(
            src_ref=CVS,
            dst_ref=CV.at[(1 + dv) * n_mem + other_m],
            send_sem=sc_send.at[(dv + 1) * n_mem + dm],
            recv_sem=sc_recv.at[(1 + dv) * n_mem + other_m],
            device_id=(me_v + dv, other_m),
            device_id_type=MESH,
        ).wait_recv()

    for dv, dm, other_m, ok in peers:
        guarded(ok, lambda a=dv, b=dm, o=other_m: cv_copy(a, b, o).start())

    def ionic(g, carry):
        for q in range(gcells):
            c = g * gcells + q
            cnt = counts[c]
            kind = jnp.full((nstates, 128), kinds[c], jnp.int32)
            tc = PB[5]
            for k in range(1, ntypes):
                tc = jnp.where(kind == k, PB[5 + k], tc)
            for h in range(fpc // 128):
                off = q * fpc + h * 128
                v = VOLT[g, :, off:off + 128]
                lanes = pl.ds(pl.multiple_of(g * gf + off, 128), 128)
                st = states[:, lanes]
                opening = PB[0] * jnp.exp(PB[1] * v)
                closing = PB[2] * jnp.exp(-(PB[3] * v))
                total = opening + closing
                steady = opening / total
                fresh = steady + (st - steady) * jnp.exp(-time_step * total)
                live = (lane1 + h * 128) < cnt
                out_states[:, lanes] = jnp.where(live, fresh, st)
                cur = jnp.sum(tc * fresh * (v - PB[4]), axis=0, keepdims=True)
                out_cur[g, :, off:off + 128] = cur
        return carry

    lax.fori_loop(0, groups, ionic, 0)

    for dv, dm, other_m, ok in peers:
        guarded(ok, lambda a=dv, b=dm, o=other_m: cv_wait(a, b, o))

    nb = 3 * n_mem
    band = jnp.concatenate([CV[i, 0:1, :] for i in range(nb)] + [jnp.zeros((-nb % 16, 128), F32)], axis=0)
    hi, mid = split2(band)
    rest = (band - hi.astype(F32) - mid.astype(F32)).astype(BF16)
    lhs = jnp.concatenate([hi, mid, rest], axis=0)
    nbr = nb + (-nb % 16)
    gap = jnp.zeros((1, cells), F32)
    for j in range(partner.shape[0]):
        pos = partner[j:j + 1, :]
        slot_row = pos // cells - (me_v - 1) * n_mem
        col = pos % cells
        table = jnp.where(lax.broadcasted_iota(jnp.int32, (128, cells), 0) == col, 1.0, 0.0).astype(BF16)
        got = jnp.dot(lhs, table, preferred_element_type=F32)
        got = got[:nbr] + got[nbr:2 * nbr] + got[2 * nbr:]
        mask = lax.broadcasted_iota(jnp.int32, (nbr, cells), 0) == slot_row
        pv = jnp.sum(jnp.where(mask, got, 0.0), axis=0, keepdims=True)
        gap = gap + gcond[j:j + 1, :] * (cell_volt[:, :cells] - pv)

    def scatter(g, carry):
        cur = []
        for q in range(gcells):
            c = g * gcells + q
            cnt = counts[c]
            share = jnp.sum(jnp.where(lane1[:, :cells] == c, gap, 0.0), axis=1, keepdims=True)
            share = share / jnp.maximum(jnp.full((1, fpc), cnt, jnp.int32), 1).astype(F32)
            ion = out_cur[g, :, q * fpc:(q + 1) * fpc]
            cur.append(jnp.where(slot_k < cnt, ion + share, 0.0))
        cur = jnp.concatenate(cur, axis=1)
        out_cur[g] = cur
        hi = cur.astype(BF16).astype(F32)
        lo = cur - hi
        source = None
        for i, ref in enumerate((intra, extra)):
            idx = ref[g]
            row = ((idx >> 7) & (zts - 1)) * 8 + ((idx // CZ) & 7)
            mask = lax.broadcasted_iota(jnp.int32, (8 * zts, gf), 0) == row
            sign = 1.0 if i == 0 else -1.0
            vals = jnp.concatenate(
                [jnp.where(mask, sign * part, 0.0).astype(BF16) for part in (hi, lo)], axis=0
            )
            put = lax.dot_general(vals, LT[g, i], (((1,), (1,)), ((), ())), preferred_element_type=F32)
            source = put if source is None else source + put
        half = source.shape[0] // 2
        source = source[:half] + source[half:]
        gx, gy = g // ybs, g % ybs
        rows = pl.ds(pl.multiple_of(gy * 8, 8), 8)
        for z in range(zts):
            R[gx, rows, z * 128:(z + 1) * 128] = source[z * 8:(z + 1) * 8, :]
        return carry

    lax.fori_loop(0, groups, scatter, 0)

    for p in range(CX):
        C[p, 8:8 + CY, :] = cond[p]
        X[0, p, 8:8 + CY, :] = pot[p]

    def put_y(dst, e):
        for p in range(CX):
            dst[p, 7:8, :] = YR[e, 0, p:p + 1, :]
            dst[p, 8 + CY:9 + CY, :] = YR[e, 1, p:p + 1, :]

    wait_y(0)
    put_y(C, 0)
    for ch in range(CHUNKS):
        wait_x(0, ch)
    lane = lax.broadcasted_iota(jnp.int32, (8, CZ), 1)
    sub = lax.broadcasted_iota(jnp.int32, (8, CZ), 0)

    def views(src, halo, p, yb):
        base = pl.multiple_of(yb * 8, 8)
        rows = pl.ds(base + 8, 8)
        own = pl.ds(base, 8)
        centre = src[p, rows, :]
        below = halo[0, own, :] if p == 0 else src[p - 1, rows, :]
        above = halo[1, own, :] if p == CX - 1 else src[p + 1, rows, :]
        before = src[p, pl.ds(base, 8), :]
        after = src[p, pl.ds(pl.multiple_of(base + 16, 8), 8), :]
        return own, centre, (
            below, above,
            pltpu.roll(jnp.where(sub == 7, before, centre), 1, 0),
            pltpu.roll(jnp.where(sub == 0, after, centre), 7, 0),
            pltpu.roll(centre, 1, 1), pltpu.roll(centre, CZ - 1, 1),
        )

    def coeffs(yb, carry):
        for p in range(CX):
            own, centre, near = views(C, HX.at[0], p, yb)
            near = list(near)
            near[4] = jnp.where(lane == 0, 0.0, near[4])
            near[5] = jnp.where(lane == CZ - 1, 0.0, near[5])
            faces = [centre + n for n in near]
            total = faces[0] + faces[1] + faces[2] + faces[3] + faces[4] + faces[5]
            inv = 1.0 / (mass_coef + (0.5 * time_step) * total)
            scale = (0.5 * time_step) * inv
            faces[4] = jnp.where(lane == 0, 0.0, faces[4])
            faces[5] = jnp.where(lane == CZ - 1, 0.0, faces[5])
            for k in range(6):
                K[k, p, own, :] = faces[k] * scale
            R[p, own, :] = (mass_coef * pot[p, own, :] - time_step * R[p, own, :]) * inv
        return carry

    lax.fori_loop(0, ybs, coeffs, 0)

    weights = sweep_weights()
    for t in range(ITERS):
        e = t + 1
        last = t == ITERS - 1
        wa, wb = weights[t]
        wait_y(e)
        put_y(X.at[t], e)

        def tile(p, yb, t=t, e=e, last=last, wa=wa, wb=wb):
            own, centre, near = views(X.at[t], HX.at[e], p, yb)
            acc = R[p, own, :] - centre
            for k in range(6):
                acc = acc + K[k, p, own, :] * near[k]
            step = wb * acc
            if t > 0:
                step = step + wa * U[p, own, :]
            new = centre + step
            if last:
                out_pot[p, own, :] = new
            else:
                U[p, own, :] = step
                X[t + 1, p, pl.ds(pl.multiple_of(yb * 8, 8) + 8, 8), :] = new

        def inner(yb, carry, tile=tile):
            for p in range(1, CX - 1):
                tile(p, yb)
            return carry

        lax.fori_loop(0, ybs, inner, 0)
        per = ybs // CHUNKS
        for ch in range(CHUNKS):
            wait_x(e, ch)

            def outer(yb, carry, tile=tile):
                tile(0, yb)
                if CX > 1:
                    tile(CX - 1, yb)
                return carry

            lax.fori_loop(ch * per, (ch + 1) * per, outer, 0)
            if not last:
                send_x(e + 1, ch)
        if not last:
            for p in range(CX):
                YS[e + 1, 0, p:p + 1, :] = X[t + 1, p, 8:9, :]
                YS[e + 1, 1, p:p + 1, :] = X[t + 1, p, 7 + CY:8 + CY, :]
            send_y(e + 1)

    for e in range(ITERS + 1):
        for side in (0, 1):
            for ch in range(CHUNKS):
                guarded(has[0][side], lambda e=e, s=side, ch=ch: x_copy(e, s, ch, face_of(e, s, ch)).wait_send())
            guarded(has[1][side], lambda e=e, s=side: y_copy(e, s).wait_send())
    for dv, dm, other_m, ok in peers:
        guarded(ok, lambda a=dv, b=dm, o=other_m: cv_copy(a, b, o).wait_send())


def per_device(
    n_vol, n_mem,
    potential, conductivity, ion_states, rate_scale, rate_slope, type_cond, reversal,
    facet_counts, intra_voxel, extra_voxel, cell_type, gap_partner, gap_cond,
):
    CX, CY, CZ = potential.shape
    nstates, facets = ion_states.shape
    cells = facet_counts.shape[0]
    ntypes = type_cond.shape[0]
    groups = CX * CY // 8
    gf = facets // groups
    ncols = 5 + ntypes
    vmem = pl.BlockSpec(memory_space=pltpu.VMEM)
    ex = ITERS + 1
    nb = 3 * n_mem
    args = (
        potential, conductivity, ion_states, rate_scale, rate_slope, type_cond, reversal[None, :],
        facet_counts, cell_type,
        intra_voxel.reshape(groups, 1, gf), extra_voxel.reshape(groups, 1, gf), gap_partner.T, gap_cond.T,
    )
    args = tuple(pltpu.with_memory_space_constraint(a, pltpu.HBM) for a in args)
    held = [
        (pltpu.SMEM if a.ndim == 1 else pltpu.VMEM)(a.shape, a.dtype) for a in args
    ]
    out = pl.pallas_call(
        functools.partial(kernel, n_vol, n_mem, ntypes),
        out_shape=(
            jax.ShapeDtypeStruct(potential.shape, F32),
            jax.ShapeDtypeStruct(ion_states.shape, F32),
            jax.ShapeDtypeStruct((groups, 1, gf), F32),
        ),
        in_specs=[pl.BlockSpec(memory_space=pltpu.HBM)] * len(args),
        out_specs=(vmem, vmem, vmem),
        scratch_shapes=held + [
            pltpu.SemaphoreType.DMA((len(args),)),
            pltpu.VMEM((ITERS, CX, CY + 16, CZ), F32),
            pltpu.VMEM((CX, CY + 16, CZ), F32),
            pltpu.VMEM((6, CX, CY, CZ), F32),
            pltpu.VMEM((CX, CY, CZ), F32),
            pltpu.VMEM((CX, CY, CZ), F32),
            pltpu.VMEM((ex, 2, CY, CZ), F32),
            pltpu.VMEM((ex, 2, 8, CZ), F32),
            pltpu.VMEM((ex, 2, 8, CZ), F32),
            pltpu.VMEM((groups, 2, 128, gf), BF16),
            pltpu.VMEM((ncols, nstates, 128), F32),
            pltpu.VMEM((groups, 1, gf), F32),
            pltpu.VMEM((8, 128), F32),
            pltpu.VMEM((nb, 8, 128), F32),
            pltpu.SemaphoreType.DMA((ex, 2, CHUNKS)),
            pltpu.SemaphoreType.DMA((ex, 2, CHUNKS)),
            pltpu.SemaphoreType.DMA((ex, 2)),
            pltpu.SemaphoreType.DMA((ex, 2)),
            pltpu.SemaphoreType.DMA((nb,)),
            pltpu.SemaphoreType.DMA((nb,)),
        ],
        compiler_params=pltpu.CompilerParams(
            collective_id=0, has_side_effects=True, vmem_limit_bytes=42 * 1024 * 1024
        ),
    )(*args)
    return out[0], out[1], out[2].reshape(-1)


def solution(mesh):
    sizes = dict(mesh.shape)
    in_specs = (
        P("vol", "mem", None),
        P("vol", "mem", None),
        P(None, ("vol", "mem")),
        P(),
        P(),
        P(),
        P(),
        P(("vol", "mem")),
        P(("vol", "mem")),
        P(("vol", "mem")),
        P(("vol", "mem")),
        P(("vol", "mem"), None),
        P(("vol", "mem"), None),
    )
    out_specs = (P("vol", "mem", None), P(None, ("vol", "mem")), P(("vol", "mem")))
    return jax.shard_map(
        functools.partial(per_device, sizes["vol"], sizes["mem"]),
        mesh=mesh, in_specs=in_specs, out_specs=out_specs, check_vma=False,
    )
```

profile of v0, /device:TPU:9, one launch (start us, length us, event | category | flops | bytes accessed | tf_op | source)
XLA Modules:
  0.0 80.9 jit_solution(9585194234758619897)
XLA Ops:
  0.6 77.1 %shard_map.148 = (f32[4,64,1024]{2,1,0:T(8,128)S(1)}, f32[40,16384]{1,0:T(8,128)S(1)}, f32[32,1,512]{2,1,0:T(1,128)S(1)}) custom-call(f32[4,64,1024]{2,1,0:T(8,128)} %refs_0_.1, f32[4,64,1024]{2,1,0:T(8,128)} %refs_1_.1, f32[40,16384]{1,0:T(8,128)} %refs_2_.1, f32[2,40]{1,0:T(2,128)} %refs_3_.1, f32[2,40]{1,0:T(2,128)} %refs_4_.1, f32[3,40]{1,0:T(4,128)} %refs_5_.1, ...), custom_call_target="tpu_custom_call" | custom-call | tf_op jit(solution)/shard_map/pallas_call | solution.py:473
  77.8 1.0 %copy.19 = f32[4,64,1024]{2,1,0:T(8,128)} copy(f32[4,64,1024]{2,1,0:T(8,128)S(1)} %get-tuple-element.12) | data formatting | bytes 2097152
  78.7 1.5 %copy.20 = f32[40,16384]{1,0:T(8,128)} copy(f32[40,16384]{1,0:T(8,128)S(1)} %get-tuple-element.13) | data formatting | bytes 5242880
  80.2 0.6 copy.21
where the time goes:
time: 81 us; the launch traced here: 80.9 us
  Pallas kernels  77.1 us (95%)
  local copies, waits for them, and re-layouts  3.1 us (4%)
    pallas_call x1, Pallas kernels, per_device(): pl.pallas_call(functools.partial(kernel, n_vol, n_mem, ntypes), out_shape...  77.1 us
    unnamed x3, local copies, waits for them, and re-layouts  3.1 us

commit v1 on v0

--- a/solution.py
+++ b/solution.py
@@ -44,34 +44,63 @@
     *refs,
 ):
     count = 13
-    given, outs, held = refs[:count], refs[count:count + 3], refs[count + 3:2 * count + 3]
-    body(n_vol, n_mem, ntypes, given, *held, *outs, *refs[2 * count + 3:])
+    body(n_vol, n_mem, ntypes, refs[:count], *refs[count:])
+
+
+def home(n_vol, n_mem, v, m):
+    if n_vol % 2 or n_mem % 2:
+        return v, m
+    d = lax.rem(m, 2) - lax.rem(v, 2)
+    return v + d, m - d
 
 
 def body(
     n_vol, n_mem, ntypes, given,
-    pot, cond, states, rate_scale, rate_slope, type_cond, reversal, counts, kinds, intra, extra, partner, gcond,
     out_pot, out_states, out_cur,
-    sl,
-    X, C, K, R, U, HX, YS, YR, LT, PB, VOLT, CVS, CV,
-    sx_send, sx_recv, sy_send, sy_recv, sc_send, sc_recv,
+    pot, states, rate_scale, rate_slope, type_cond, reversal, counts, kinds, partner, gcond,
+    sl, IN, EX, CUR, EDGE,
+    X, C, K, R, U, HX, YS, YR, PB, VOLT, CVS, CV,
+    sx_send, sx_recv, sy_send, sy_recv, sc_send, sc_recv, sb_send, sb_recv, st_send, st_recv, sr_send, sr_recv,
 ):
-    held = (pot, cond, states, rate_scale, rate_slope, type_cond, reversal, counts, kinds, intra, extra, partner, gcond)
-    loads = [pltpu.make_async_copy(src, dst, sl.at[i]) for i, (src, dst) in enumerate(zip(given, held))]
-    for i in (1, 0, 9, 10, 7, 8, 3, 4, 5, 6, 2, 11, 12):
-        loads[i].start()
     CX, CY, CZ = pot.shape
     nstates, facets = states.shape
     cells = counts.shape[0]
     fpc = facets // cells
-    groups, _, gf = intra.shape
+    groups, _, gf = IN.shape[1:]
     gcells = gf // fpc
     ybs = CY // 8
     zts = CZ // 128
     crow = CY // CHUNKS
+    g_pot, g_cond, g_states, g_rs, g_rl, g_tc, g_rev, g_cnt, g_kind, g_in, g_ex, g_part, g_gc = given
+    pairs = (
+        (g_pot, pot), (g_in, IN.at[0]), (g_ex, EX.at[0]), (g_cnt, counts), (g_kind, kinds),
+        (g_cond.at[:, pl.ds(0, 8)], EDGE.at[0]), (g_cond.at[:, pl.ds(CY - 8, 8)], EDGE.at[1]),
+        (g_rs, rate_scale), (g_rl, rate_slope), (g_tc, type_cond), (g_rev, reversal), (g_states, states),
+        (g_part, partner), (g_gc, gcond),
+    )
+    loads = [pltpu.make_async_copy(src, dst, sl.at[i]) for i, (src, dst) in enumerate(pairs)]
+    for load in loads:
+        load.start()
     me_v = lax.axis_index("vol")
     me_m = lax.axis_index("mem")
-    has = ((me_v > 0, me_v < n_vol - 1), (me_m > 0, me_m < n_mem - 1))
+    trades = n_vol % 2 == 0 and n_mem % 2 == 0
+    role_v, role_m = home(n_vol, n_mem, me_v, me_m)
+    away = role_v != me_v
+    stays = role_v == me_v
+    sel = away.astype(jnp.int32)
+    own = ((me_v > 0, me_v < n_vol - 1), (me_m > 0, me_m < n_mem - 1))
+    has = ((role_v > 0, role_v < n_vol - 1), (role_m > 0, role_m < n_mem - 1))
+
+    def x_peer(side):
+        return home(n_vol, n_mem, role_v + (1 if side else -1), role_m)
+
+    def y_peer(e, side):
+        if e < 2:
+            return home(n_vol, n_mem, me_v, me_m + (1 if side else -1))
+        return home(n_vol, n_mem, role_v, role_m + (1 if side else -1))
+
+    def y_ok(e, side):
+        return (own if e < 2 else has)[1][side]
 
     peers = []
     for dv in (-1, 0, 1):
@@ -79,7 +108,7 @@
             if dv == 0 and dm == 0:
                 continue
             other_m = lax.rem(me_m + dm, n_mem)
-            ok = None if dv == 0 else has[0][0 if dv < 0 else 1]
+            ok = None if dv == 0 else own[0][0 if dv < 0 else 1]
             peers.append((dv, dm, other_m, ok))
 
     def guarded(ok, fn):
@@ -93,8 +122,93 @@
         def greet(dv=dv, other_m=other_m):
             pl.semaphore_signal(barrier, inc=1, device_id=(me_v + dv, other_m), device_id_type=MESH)
         guarded(ok, greet)
-    columns = 1 + has[0][0].astype(jnp.int32) + has[0][1].astype(jnp.int32)
-    pl.semaphore_wait(barrier, columns * n_mem - 1)
+    columns = 1 + own[0][0].astype(jnp.int32) + own[0][1].astype(jnp.int32)
+    expected = columns * n_mem - 1
+    if trades:
+        odd = lax.rem(me_m, 2)
+        far_v, far_m = me_v + 4 * odd - 2, me_m + 1 - 2 * odd
+        far_ok = jnp.logical_and(far_v >= 0, far_v < n_vol)
+
+        @pl.when(far_ok)
+        def _():
+            pl.semaphore_signal(barrier, inc=1, device_id=(far_v, far_m), device_id_type=MESH)
+        expected = expected + far_ok.astype(jnp.int32)
+    pl.semaphore_wait(barrier, expected)
+
+    order = [0] + ([CX - 1] if CX > 1 else []) + list(range(1, CX - 1))
+
+    def bulk_refs(e, p):
+        return (g_cond, g_pot)[e].at[p], (C if e == 0 else X.at[0]).at[p, pl.ds(8, CY)]
+
+    def bulk_far(e, p):
+        src, dst = bulk_refs(e, p)
+        return pltpu.make_async_remote_copy(
+            src_ref=src, dst_ref=dst, send_sem=sb_send.at[e, p], recv_sem=sb_recv.at[e, p],
+            device_id=(role_v, role_m), device_id_type=MESH,
+        )
+
+    def bulk_near(e, p):
+        src, dst = bulk_refs(e, p)
+        return pltpu.make_async_copy(src, dst, sb_recv.at[e, p])
+
+    def table_far(k):
+        src, dst = ((g_in, IN.at[1]), (g_ex, EX.at[1]), (CUR.at[0], CUR.at[1]))[k]
+        return pltpu.make_async_remote_copy(
+            src_ref=src, dst_ref=dst, send_sem=st_send.at[k], recv_sem=st_recv.at[k],
+            device_id=(role_v, role_m), device_id_type=MESH,
+        )
+
+    def back_far(p, ch):
+        rows = pl.ds(ch * crow, crow)
+        return pltpu.make_async_remote_copy(
+            src_ref=X.at[0, p, pl.ds(8 + ch * crow, crow)], dst_ref=out_pot.at[p, rows],
+            send_sem=sr_send.at[p, ch], recv_sem=sr_recv.at[p, ch],
+            device_id=(role_v, role_m), device_id_type=MESH,
+        )
+
+    def back_near(p, ch):
+        rows = pl.ds(ch * crow, crow)
+        return pltpu.make_async_copy(
+            X.at[0, p, pl.ds(8 + ch * crow, crow)], out_pot.at[p, rows], sr_recv.at[p, ch]
+        )
+
+    def either(far, near):
+        if trades:
+            pl.when(away)(far)
+            pl.when(stays)(near)
+        else:
+            near()
+
+    def bulk_start():
+        edge, inner = order[:2], order[2:]
+
+        def far():
+            for e in (0, 1):
+                for p in edge:
+                    bulk_far(e, p).start()
+            table_far(0).start()
+            table_far(1).start()
+            for e in (0, 1):
+                for p in inner:
+                    bulk_far(e, p).start()
+
+        def near():
+            for e in (0, 1):
+                for p in order:
+                    bulk_near(e, p).start()
+        either(far, near)
+
+    def bulk_wait(e, planes):
+        def far():
+            for p in planes:
+                bulk_far(e, p).wait_recv()
+
+        def near():
+            for p in planes:
+                bulk_near(e, p).wait()
+        either(far, near)
+
+    bulk_start()
 
     def x_copy(e, side, ch, plane_ref):
         rows = pl.ds(ch * crow, crow)
@@ -103,7 +217,7 @@
             dst_ref=HX.at[e, 1 - side, rows],
             send_sem=sx_send.at[e, side, ch],
             recv_sem=sx_recv.at[e, 1 - side, ch],
-            device_id=(me_v + (1 if side else -1), me_m),
+            device_id=x_peer(side),
             device_id_type=MESH,
         )
 
@@ -113,17 +227,14 @@
             dst_ref=YR.at[e, 1 - side],
             send_sem=sy_send.at[e, side],
             recv_sem=sy_recv.at[e, 1 - side],
-            device_id=(me_v, me_m + (1 if side else -1)),
+            device_id=y_peer(e, side),
             device_id_type=MESH,
         )
 
     def face_of(e, side, ch):
         plane = CX - 1 if side else 0
-        if e == 0:
-            return cond.at[plane, pl.ds(ch * crow, crow)]
-        if e == 1:
-            return pot.at[plane, pl.ds(ch * crow, crow)]
-        return X.at[e - 1, plane, pl.ds(8 + ch * crow, crow)]
+        src = C if e == 0 else X.at[e - 1]
+        return src.at[plane, pl.ds(8 + ch * crow, crow)]
 
     def send_x(e, ch):
         for side in (0, 1):
@@ -137,14 +248,14 @@
                     dst_ref=HX.at[e, side, pl.ds(ch * crow, crow)],
                     send_sem=sx_send.at[e, side, ch],
                     recv_sem=sx_recv.at[e, side, ch],
-                    device_id=(me_v + (1 if side else -1), me_m),
+                    device_id=x_peer(side),
                     device_id_type=MESH,
                 ).wait_recv()
             guarded(has[0][side], w)
 
     def send_y(e):
         for side in (0, 1):
-            guarded(has[1][side], lambda side=side: y_copy(e, side).start())
+            guarded(y_ok(e, side), lambda side=side: y_copy(e, side).start())
 
     def wait_y(e):
         for side in (0, 1):
@@ -154,23 +265,22 @@
                     dst_ref=YR.at[e, side],
                     send_sem=sy_send.at[e, side],
                     recv_sem=sy_recv.at[e, side],
-                    device_id=(me_v, me_m + (1 if side else -1)),
+                    device_id=y_peer(2, side),
                     device_id_type=MESH,
                 ).wait_recv()
             guarded(has[1][side], w)
 
+    for load in loads:
+        load.wait()
     for e in (0, 1):
-        ref = (cond, pot)[e]
-        loads[1 - e].wait()
-        for ch in range(CHUNKS):
-            send_x(e, ch)
         for p in range(CX):
-            YS[e, 0, p:p + 1, :] = ref[p, 0:1, :]
-            YS[e, 1, p:p + 1, :] = ref[p, CY - 1:CY, :]
+            if e == 0:
+                YS[e, 0, p:p + 1, :] = EDGE[0, p, 0:1, :]
+                YS[e, 1, p:p + 1, :] = EDGE[1, p, 7:8, :]
+            else:
+                YS[e, 0, p:p + 1, :] = pot[p, 0:1, :]
+                YS[e, 1, p:p + 1, :] = pot[p, CY - 1:CY, :]
         send_y(e)
-
-    for i in range(2, len(loads)):
-        loads[i].wait()
 
     for side in (0, 1):
         @pl.when(jnp.logical_not(has[0][side]))
@@ -180,6 +290,9 @@
                     HX[e, side, pl.ds(pl.multiple_of(i * 8, 8), 8), :] = jnp.zeros((8, CZ), F32)
                 return c
             lax.fori_loop(0, ybs, zero, 0)
+
+        @pl.when(jnp.logical_not(own[0][side]))
+        def _(side=side):
             for dm in range(n_mem):
                 CV[(2 if side else 0) * n_mem + dm] = jnp.zeros((8, 128), F32)
 
@@ -207,13 +320,12 @@
         hi, lo = split2(block)
         lhs = jnp.concatenate([hi, lo], axis=0)
         picked = []
-        for i, ref in enumerate((intra, extra)):
-            idx = ref[g]
+        for i, ref in enumerate((IN, EX)):
+            idx = ref[0, g]
             lane = idx & 127
             row = ((idx >> 7) & (zts - 1)) * 8 + ((idx // CZ) & 7)
             hot = lax.broadcasted_iota(jnp.int32, (128, gf), 0) == lane
             table = jnp.where(hot, 1.0, 0.0).astype(BF16)
-            LT[g, i] = table
             got = jnp.dot(lhs, table, preferred_element_type=F32)
             half = got.shape[0] // 2
             got = got[:half] + got[half:]
@@ -283,6 +395,11 @@
 
     lax.fori_loop(0, groups, ionic, 0)
 
+    for e in (0, 1):
+        bulk_wait(e, order[:2])
+        for ch in range(CHUNKS):
+            send_x(e, ch)
+
     for dv, dm, other_m, ok in peers:
         guarded(ok, lambda a=dv, b=dm, o=other_m: cv_wait(a, b, o))
 
@@ -304,7 +421,7 @@
         pv = jnp.sum(jnp.where(mask, got, 0.0), axis=0, keepdims=True)
         gap = gap + gcond[j:j + 1, :] * (cell_volt[:, :cells] - pv)
 
-    def scatter(g, carry):
+    def finish(g, carry):
         cur = []
         for q in range(gcells):
             c = g * gcells + q
@@ -315,18 +432,34 @@
             cur.append(jnp.where(slot_k < cnt, ion + share, 0.0))
         cur = jnp.concatenate(cur, axis=1)
         out_cur[g] = cur
+        CUR[0, g] = cur
+        return carry
+
+    lax.fori_loop(0, groups, finish, 0)
+    if trades:
+        @pl.when(away)
+        def _():
+            table_far(2).start()
+            for k in range(3):
+                table_far(k).wait_recv()
+
+    def scatter(g, carry):
+        cur = CUR[sel, g]
         hi = cur.astype(BF16).astype(F32)
         lo = cur - hi
         source = None
-        for i, ref in enumerate((intra, extra)):
-            idx = ref[g]
+        for i, ref in enumerate((IN, EX)):
+            idx = ref[sel, g]
+            lane = idx & 127
+            hot = lax.broadcasted_iota(jnp.int32, (128, gf), 0) == lane
+            table = jnp.where(hot, 1.0, 0.0).astype(BF16)
             row = ((idx >> 7) & (zts - 1)) * 8 + ((idx // CZ) & 7)
             mask = lax.broadcasted_iota(jnp.int32, (8 * zts, gf), 0) == row
             sign = 1.0 if i == 0 else -1.0
             vals = jnp.concatenate(
                 [jnp.where(mask, sign * part, 0.0).astype(BF16) for part in (hi, lo)], axis=0
             )
-            put = lax.dot_general(vals, LT[g, i], (((1,), (1,)), ((), ())), preferred_element_type=F32)
+            put = lax.dot_general(vals, table, (((1,), (1,)), ((), ())), preferred_element_type=F32)
             source = put if source is None else source + put
         half = source.shape[0] // 2
         source = source[:half] + source[half:]
@@ -338,9 +471,8 @@
 
     lax.fori_loop(0, groups, scatter, 0)
 
-    for p in range(CX):
-        C[p, 8:8 + CY, :] = cond[p]
-        X[0, p, 8:8 + CY, :] = pot[p]
+    for e in (0, 1):
+        bulk_wait(e, order[2:])
 
     def put_y(dst, e):
         for p in range(CX):
@@ -384,16 +516,30 @@
             faces[5] = jnp.where(lane == CZ - 1, 0.0, faces[5])
             for k in range(6):
                 K[k, p, own, :] = faces[k] * scale
-            R[p, own, :] = (mass_coef * pot[p, own, :] - time_step * R[p, own, :]) * inv
+            R[p, own, :] = (mass_coef * X[0, p, pl.ds(pl.multiple_of(yb * 8, 8) + 8, 8), :] - time_step * R[p, own, :]) * inv
         return carry
 
     lax.fori_loop(0, ybs, coeffs, 0)
+
+    def back_start(planes, ch):
+        def far():
+            for p in planes:
+                back_far(p, ch).start()
+
+        def near():
+            for p in planes:
+                back_near(p, ch).start()
+        either(far, near)
 
     weights = sweep_weights()
     for t in range(ITERS):
         e = t + 1
         last = t == ITERS - 1
         wa, wb = weights[t]
+        if last:
+            for side in (0, 1):
+                for ch in range(CHUNKS):
+                    guarded(has[0][side], lambda s=side, ch=ch: x_copy(1, s, ch, face_of(1, s, ch)).wait_send())
         wait_y(e)
         put_y(X.at[t], e)
 
@@ -406,19 +552,22 @@
             if t > 0:
                 step = step + wa * U[p, own, :]
             new = centre + step
-            if last:
-                out_pot[p, own, :] = new
-            else:
+            if not last:
                 U[p, own, :] = step
-                X[t + 1, p, pl.ds(pl.multiple_of(yb * 8, 8) + 8, 8), :] = new
+            X[(t + 1) % ITERS, p, pl.ds(pl.multiple_of(yb * 8, 8) + 8, 8), :] = new
 
         def inner(yb, carry, tile=tile):
             for p in range(1, CX - 1):
                 tile(p, yb)
             return carry
 
-        lax.fori_loop(0, ybs, inner, 0)
         per = ybs // CHUNKS
+        if last:
+            for ch in range(CHUNKS):
+                lax.fori_loop(ch * per, (ch + 1) * per, inner, 0)
+                back_start(range(1, CX - 1), ch)
+        else:
+            lax.fori_loop(0, ybs, inner, 0)
         for ch in range(CHUNKS):
             wait_x(e, ch)
 
@@ -429,7 +578,9 @@
                 return carry
 
             lax.fori_loop(ch * per, (ch + 1) * per, outer, 0)
-            if not last:
+            if last:
+                back_start(order[:2], ch)
+            else:
                 send_x(e + 1, ch)
         if not last:
             for p in range(CX):
@@ -439,11 +590,27 @@
 
     for e in range(ITERS + 1):
         for side in (0, 1):
-            for ch in range(CHUNKS):
+            for ch in range(CHUNKS if e != 1 else 0):
                 guarded(has[0][side], lambda e=e, s=side, ch=ch: x_copy(e, s, ch, face_of(e, s, ch)).wait_send())
-            guarded(has[1][side], lambda e=e, s=side: y_copy(e, s).wait_send())
+            guarded(y_ok(e, side), lambda e=e, s=side: y_copy(e, s).wait_send())
     for dv, dm, other_m, ok in peers:
         guarded(ok, lambda a=dv, b=dm, o=other_m: cv_copy(a, b, o).wait_send())
+
+    def drain_far():
+        for e in (0, 1):
+            for p in range(CX):
+                bulk_far(e, p).wait_send()
+        for k in range(3):
+            table_far(k).wait_send()
+        for p in range(CX):
+            for ch in range(CHUNKS):
+                back_far(p, ch).wait()
+
+    def drain_near():
+        for p in range(CX):
+            for ch in range(CHUNKS):
+                back_near(p, ch).wait()
+    either(drain_far, drain_near)
 
 
 def per_device(
@@ -468,7 +635,8 @@
     )
     args = tuple(pltpu.with_memory_space_constraint(a, pltpu.HBM) for a in args)
     held = [
-        (pltpu.SMEM if a.ndim == 1 else pltpu.VMEM)(a.shape, a.dtype) for a in args
+        (pltpu.SMEM if a.ndim == 1 else pltpu.VMEM)(a.shape, a.dtype)
+        for i, a in enumerate(args) if i not in (1, 9, 10)
     ]
     out = pl.pallas_call(
         functools.partial(kernel, n_vol, n_mem, ntypes),
@@ -480,7 +648,11 @@
         in_specs=[pl.BlockSpec(memory_space=pltpu.HBM)] * len(args),
         out_specs=(vmem, vmem, vmem),
         scratch_shapes=held + [
-            pltpu.SemaphoreType.DMA((len(args),)),
+            pltpu.SemaphoreType.DMA((14,)),
+            pltpu.VMEM((2, groups, 1, gf), jnp.int32),
+            pltpu.VMEM((2, groups, 1, gf), jnp.int32),
+            pltpu.VMEM((2, groups, 1, gf), F32),
+            pltpu.VMEM((2, CX, 8, CZ), F32),
             pltpu.VMEM((ITERS, CX, CY + 16, CZ), F32),
             pltpu.VMEM((CX, CY + 16, CZ), F32),
             pltpu.VMEM((6, CX, CY, CZ), F32),
@@ -489,7 +661,6 @@
             pltpu.VMEM((ex, 2, CY, CZ), F32),
             pltpu.VMEM((ex, 2, 8, CZ), F32),
             pltpu.VMEM((ex, 2, 8, CZ), F32),
-            pltpu.VMEM((groups, 2, 128, gf), BF16),
             pltpu.VMEM((ncols, nstates, 128), F32),
             pltpu.VMEM((groups, 1, gf), F32),
             pltpu.VMEM((8, 128), F32),
@@ -500,6 +671,12 @@
             pltpu.SemaphoreType.DMA((ex, 2)),
             pltpu.SemaphoreType.DMA((nb,)),
             pltpu.SemaphoreType.DMA((nb,)),
+            pltpu.SemaphoreType.DMA((2, CX)),
+            pltpu.SemaphoreType.DMA((2, CX)),
+            pltpu.SemaphoreType.DMA((3,)),
+            pltpu.SemaphoreType.DMA((3,)),
+            pltpu.SemaphoreType.DMA((CX, CHUNKS)),
+            pltpu.SemaphoreType.DMA((CX, CHUNKS)),
         ],
         compiler_params=pltpu.CompilerParams(
             collective_id=0, has_side_effects=True, vmem_limit_bytes=42 * 1024 * 1024

time: 81 us -> 80.2 us (level)
  Pallas kernels: 77.1 us -> 75.9 us
    pallas_call x1, Pallas kernels: 77.1 us -> 75.9 us  [per_device(): pl.pallas_call(functools.partial(kernel, n_vol, n_mem, ntypes), out_shape...]
where the time goes in v1:
time: 80.2 us; the launch traced here: 79.6 us
  Pallas kernels  75.9 us (95%)
  local copies, waits for them, and re-layouts  3.1 us (4%)
    pallas_call x1, Pallas kernels, per_device(): pl.pallas_call(functools.partial(kernel, n_vol, n_mem, ntypes), out_shape...  75.9 us
    unnamed x3, local copies, waits for them, and re-layouts  3.1 us

profile of v1, /device:TPU:9, one launch (start us, length us, event | category | flops | bytes accessed | tf_op | source)
XLA Modules:
  0.0 79.6 jit_solution(18332569550880386460)
XLA Ops:
  0.6 75.9 %shard_map.148 = (f32[4,64,1024]{2,1,0:T(8,128)S(1)}, f32[40,16384]{1,0:T(8,128)S(1)}, f32[32,1,512]{2,1,0:T(1,128)S(1)}) custom-call(f32[4,64,1024]{2,1,0:T(8,128)} %refs_0_.1, f32[4,64,1024]{2,1,0:T(8,128)} %refs_1_.1, f32[40,16384]{1,0:T(8,128)} %refs_2_.1, f32[2,40]{1,0:T(2,128)} %refs_3_.1, f32[2,40]{1,0:T(2,128)} %refs_4_.1, f32[3,40]{1,0:T(4,128)} %refs_5_.1, ...), custom_call_target="tpu_custom_call" | custom-call | tf_op jit(solution)/shard_map/pallas_call | solution.py:641
  76.5 1.0 %copy.19 = f32[4,64,1024]{2,1,0:T(8,128)} copy(f32[4,64,1024]{2,1,0:T(8,128)S(1)} %get-tuple-element.12) | data formatting | bytes 2097152
  77.5 1.5 %copy.20 = f32[40,16384]{1,0:T(8,128)} copy(f32[40,16384]{1,0:T(8,128)S(1)} %get-tuple-element.13) | data formatting | bytes 5242880
  79.0 0.6 copy.21

commit v2 on v1

--- a/solution.py
+++ b/solution.py
@@ -8,7 +8,7 @@
 from jax.sharding import PartitionSpec as P
 
 ITERS = 4
-CHUNKS = 4
+PARTS = 3
 
 mass_coef = 1.0
 time_step = 0.5
@@ -31,6 +31,15 @@
         pairs.append((rho_next * rho, 2.0 * rho_next / delta))
         rho = rho_next
     return pairs
+
+
+def row_spans(rows):
+    if rows == 8:
+        return [(0, 8)]
+    blocks = rows // 8 - 2
+    parts = max(1, min(PARTS, blocks))
+    cuts = [8 + 8 * (blocks * i // parts) for i in range(parts + 1)]
+    return [(0, 8), (rows - 8, 8)] + [(a, b - a) for a, b in zip(cuts, cuts[1:]) if b > a]
 
 
 def split2(x):
@@ -70,7 +79,8 @@
     gcells = gf // fpc
     ybs = CY // 8
     zts = CZ // 128
-    crow = CY // CHUNKS
+    spans = row_spans(CY)
+    edges = 1 if ybs == 1 else 2
     g_pot, g_cond, g_states, g_rs, g_rl, g_tc, g_rev, g_cnt, g_kind, g_in, g_ex, g_part, g_gc = given
     pairs = (
         (g_pot, pot), (g_in, IN.at[0]), (g_ex, EX.at[0]), (g_cnt, counts), (g_kind, kinds),
@@ -159,17 +169,19 @@
         )
 
     def back_far(p, ch):
-        rows = pl.ds(ch * crow, crow)
+        start, size = spans[ch]
+        rows = pl.ds(start, size)
         return pltpu.make_async_remote_copy(
-            src_ref=X.at[0, p, pl.ds(8 + ch * crow, crow)], dst_ref=out_pot.at[p, rows],
+            src_ref=X.at[0, p, pl.ds(8 + start, size)], dst_ref=out_pot.at[p, rows],
             send_sem=sr_send.at[p, ch], recv_sem=sr_recv.at[p, ch],
             device_id=(role_v, role_m), device_id_type=MESH,
         )
 
     def back_near(p, ch):
-        rows = pl.ds(ch * crow, crow)
+        start, size = spans[ch]
+        rows = pl.ds(start, size)
         return pltpu.make_async_copy(
-            X.at[0, p, pl.ds(8 + ch * crow, crow)], out_pot.at[p, rows], sr_recv.at[p, ch]
+            X.at[0, p, pl.ds(8 + start, size)], out_pot.at[p, rows], sr_recv.at[p, ch]
         )
 
     def either(far, near):
@@ -179,23 +191,20 @@
         else:
             near()
 
-    def bulk_start():
+    def bulk_start(step):
         edge, inner = order[:2], order[2:]
+        batch = ([(0, p) for p in edge], [(1, p) for p in edge], [(e, p) for e in (0, 1) for p in inner])[step]
 
         def far():
-            for e in (0, 1):
-                for p in edge:
-                    bulk_far(e, p).start()
-            table_far(0).start()
-            table_far(1).start()
-            for e in (0, 1):
-                for p in inner:
-                    bulk_far(e, p).start()
+            for e, p in batch:
+                bulk_far(e, p).start()
+            if step == 0:
+                table_far(0).start()
+                table_far(1).start()
 
         def near():
-            for e in (0, 1):
-                for p in order:
-                    bulk_near(e, p).start()
+            for e, p in batch:
+                bulk_near(e, p).start()
         either(far, near)
 
     def bulk_wait(e, planes):
@@ -208,10 +217,10 @@
                 bulk_near(e, p).wait()
         either(far, near)
 
-    bulk_start()
+    bulk_start(0)
 
     def x_copy(e, side, ch, plane_ref):
-        rows = pl.ds(ch * crow, crow)
+        rows = pl.ds(*spans[ch])
         return pltpu.make_async_remote_copy(
             src_ref=plane_ref,
             dst_ref=HX.at[e, 1 - side, rows],
@@ -234,7 +243,7 @@
     def face_of(e, side, ch):
         plane = CX - 1 if side else 0
         src = C if e == 0 else X.at[e - 1]
-        return src.at[plane, pl.ds(8 + ch * crow, crow)]
+        return src.at[plane, pl.ds(8 + spans[ch][0], spans[ch][1])]
 
     def send_x(e, ch):
         for side in (0, 1):
@@ -244,8 +253,8 @@
         for side in (0, 1):
             def w(side=side):
                 pltpu.make_async_remote_copy(
-                    src_ref=HX.at[e, side, pl.ds(ch * crow, crow)],
-                    dst_ref=HX.at[e, side, pl.ds(ch * crow, crow)],
+                    src_ref=HX.at[e, side, pl.ds(*spans[ch])],
+                    dst_ref=HX.at[e, side, pl.ds(*spans[ch])],
                     send_sem=sx_send.at[e, side, ch],
                     recv_sem=sx_recv.at[e, side, ch],
                     device_id=x_peer(side),
@@ -270,8 +279,10 @@
                 ).wait_recv()
             guarded(has[1][side], w)
 
-    for load in loads:
-        load.wait()
+    late = 11
+    for i, load in enumerate(loads):
+        if i != late:
+            load.wait()
     for e in (0, 1):
         for p in range(CX):
             if e == 0:
@@ -368,6 +379,8 @@
 
     for dv, dm, other_m, ok in peers:
         guarded(ok, lambda a=dv, b=dm, o=other_m: cv_copy(a, b, o).start())
+    bulk_start(1)
+    loads[late].wait()
 
     def ionic(g, carry):
         for q in range(gcells):
@@ -395,11 +408,6 @@
 
     lax.fori_loop(0, groups, ionic, 0)
 
-    for e in (0, 1):
-        bulk_wait(e, order[:2])
-        for ch in range(CHUNKS):
-            send_x(e, ch)
-
     for dv, dm, other_m, ok in peers:
         guarded(ok, lambda a=dv, b=dm, o=other_m: cv_wait(a, b, o))
 
@@ -440,6 +448,14 @@
         @pl.when(away)
         def _():
             table_far(2).start()
+    bulk_start(2)
+    for e in (0, 1):
+        bulk_wait(e, order[:2])
+        for ch in range(len(spans)):
+            send_x(e, ch)
+    if trades:
+        @pl.when(away)
+        def _():
             for k in range(3):
                 table_far(k).wait_recv()
 
@@ -481,7 +497,7 @@
 
     wait_y(0)
     put_y(C, 0)
-    for ch in range(CHUNKS):
+    for ch in range(len(spans)):
         wait_x(0, ch)
     lane = lax.broadcasted_iota(jnp.int32, (8, CZ), 1)
     sub = lax.broadcasted_iota(jnp.int32, (8, CZ), 0)
@@ -538,10 +554,8 @@
         wa, wb = weights[t]
         if last:
             for side in (0, 1):
-                for ch in range(CHUNKS):
+                for ch in range(len(spans)):
                     guarded(has[0][side], lambda s=side, ch=ch: x_copy(1, s, ch, face_of(1, s, ch)).wait_send())
-        wait_y(e)
-        put_y(X.at[t], e)
 
         def tile(p, yb, t=t, e=e, last=last, wa=wa, wb=wb):
             own, centre, near = views(X.at[t], HX.at[e], p, yb)
@@ -556,41 +570,46 @@
                 U[p, own, :] = step
             X[(t + 1) % ITERS, p, pl.ds(pl.multiple_of(yb * 8, 8) + 8, 8), :] = new
 
-        def inner(yb, carry, tile=tile):
-            for p in range(1, CX - 1):
-                tile(p, yb)
-            return carry
-
-        per = ybs // CHUNKS
-        if last:
-            for ch in range(CHUNKS):
-                lax.fori_loop(ch * per, (ch + 1) * per, inner, 0)
-                back_start(range(1, CX - 1), ch)
-        else:
-            lax.fori_loop(0, ybs, inner, 0)
-        for ch in range(CHUNKS):
+        def sweep(planes, ch, tile=tile):
+            def at(yb, carry):
+                for p in planes:
+                    tile(p, yb)
+                return carry
+            start, size = spans[ch]
+            if size == 8:
+                at(start // 8, 0)
+            else:
+                lax.fori_loop(start // 8, (start + size) // 8, at, 0)
+
+        middle, faces = range(1, CX - 1), order[:2]
+        for ch in range(edges, len(spans)):
+            sweep(middle, ch)
+            if last:
+                back_start(middle, ch)
+        wait_y(e)
+        put_y(X.at[t], e)
+        for ch in range(edges):
+            sweep(middle, ch)
+            if last:
+                back_start(middle, ch)
+        for ch in range(len(spans)):
             wait_x(e, ch)
-
-            def outer(yb, carry, tile=tile):
-                tile(0, yb)
-                if CX > 1:
-                    tile(CX - 1, yb)
-                return carry
-
-            lax.fori_loop(ch * per, (ch + 1) * per, outer, 0)
+            sweep(faces, ch)
             if last:
-                back_start(order[:2], ch)
-            else:
+                back_start(faces, ch)
+            elif ch == edges - 1:
+                for p in range(CX):
+                    YS[e + 1, 0, p:p + 1, :] = X[t + 1, p, 8:9, :]
+                    YS[e + 1, 1, p:p + 1, :] = X[t + 1, p, 7 + CY:8 + CY, :]
+                send_y(e + 1)
+                for k in range(edges):
+                    send_x(e + 1, k)
+            elif ch >= edges:
                 send_x(e + 1, ch)
-        if not last:
-            for p in range(CX):
-                YS[e + 1, 0, p:p + 1, :] = X[t + 1, p, 8:9, :]
-                YS[e + 1, 1, p:p + 1, :] = X[t + 1, p, 7 + CY:8 + CY, :]
-            send_y(e + 1)
 
     for e in range(ITERS + 1):
         for side in (0, 1):
-            for ch in range(CHUNKS if e != 1 else 0):
+            for ch in range(len(spans) if e != 1 else 0):
                 guarded(has[0][side], lambda e=e, s=side, ch=ch: x_copy(e, s, ch, face_of(e, s, ch)).wait_send())
             guarded(y_ok(e, side), lambda e=e, s=side: y_copy(e, s).wait_send())
     for dv, dm, other_m, ok in peers:
@@ -603,12 +622,12 @@
         for k in range(3):
             table_far(k).wait_send()
         for p in range(CX):
-            for ch in range(CHUNKS):
+            for ch in range(len(spans)):
                 back_far(p, ch).wait()
 
     def drain_near():
         for p in range(CX):
-            for ch in range(CHUNKS):
+            for ch in range(len(spans)):
                 back_near(p, ch).wait()
     either(drain_far, drain_near)
 
@@ -627,6 +646,7 @@
     ncols = 5 + ntypes
     vmem = pl.BlockSpec(memory_space=pltpu.VMEM)
     ex = ITERS + 1
+    spans = len(row_spans(CY))
     nb = 3 * n_mem
     args = (
         potential, conductivity, ion_states, rate_scale, rate_slope, type_cond, reversal[None, :],
@@ -665,8 +685,8 @@
             pltpu.VMEM((groups, 1, gf), F32),
             pltpu.VMEM((8, 128), F32),
             pltpu.VMEM((nb, 8, 128), F32),
-            pltpu.SemaphoreType.DMA((ex, 2, CHUNKS)),
-            pltpu.SemaphoreType.DMA((ex, 2, CHUNKS)),
+            pltpu.SemaphoreType.DMA((ex, 2, spans)),
+            pltpu.SemaphoreType.DMA((ex, 2, spans)),
             pltpu.SemaphoreType.DMA((ex, 2)),
             pltpu.SemaphoreType.DMA((ex, 2)),
             pltpu.SemaphoreType.DMA((nb,)),
@@ -675,8 +695,8 @@
             pltpu.SemaphoreType.DMA((2, CX)),
             pltpu.SemaphoreType.DMA((3,)),
             pltpu.SemaphoreType.DMA((3,)),
-            pltpu.SemaphoreType.DMA((CX, CHUNKS)),
-            pltpu.SemaphoreType.DMA((CX, CHUNKS)),
+            pltpu.SemaphoreType.DMA((CX, spans)),
+            pltpu.SemaphoreType.DMA((CX, spans)),
         ],
         compiler_params=pltpu.CompilerParams(
             collective_id=0, has_side_effects=True, vmem_limit_bytes=42 * 1024 * 1024

time: 80.2 us -> 65.5 us (0.82)
  Pallas kernels: 75.9 us -> 60.9 us
    pallas_call x1, Pallas kernels: 75.9 us -> 60.9 us  [per_device(): pl.pallas_call(functools.partial(kernel, n_vol, n_mem, ntypes), out_shape...]
where the time goes in v2:
time: 65.5 us; the launch traced here: 64.6 us
  Pallas kernels  60.9 us (93%)
  local copies, waits for them, and re-layouts  3.1 us (5%)
    pallas_call x1, Pallas kernels, per_device(): pl.pallas_call(functools.partial(kernel, n_vol, n_mem, ntypes), out_shape...  60.9 us
    unnamed x3, local copies, waits for them, and re-layouts  3.1 us

profile of v2, /device:TPU:9, one launch (start us, length us, event | category | flops | bytes accessed | tf_op | source)
XLA Modules:
  0.0 64.6 jit_solution(14807257729854960407)
XLA Ops:
  0.6 60.9 %shard_map.148 = (f32[4,64,1024]{2,1,0:T(8,128)S(1)}, f32[40,16384]{1,0:T(8,128)S(1)}, f32[32,1,512]{2,1,0:T(1,128)S(1)}) custom-call(f32[4,64,1024]{2,1,0:T(8,128)} %refs_0_.1, f32[4,64,1024]{2,1,0:T(8,128)} %refs_1_.1, f32[40,16384]{1,0:T(8,128)} %refs_2_.1, f32[2,40]{1,0:T(2,128)} %refs_3_.1, f32[2,40]{1,0:T(2,128)} %refs_4_.1, f32[3,40]{1,0:T(4,128)} %refs_5_.1, ...), custom_call_target="tpu_custom_call" | custom-call | tf_op jit(solution)/shard_map/pallas_call | solution.py:661
  61.5 1.0 %copy.19 = f32[4,64,1024]{2,1,0:T(8,128)} copy(f32[4,64,1024]{2,1,0:T(8,128)S(1)} %get-tuple-element.12) | data formatting | bytes 2097152
  62.5 1.5 %copy.20 = f32[40,16384]{1,0:T(8,128)} copy(f32[40,16384]{1,0:T(8,128)S(1)} %get-tuple-element.13) | data formatting | bytes 5242880
  64.0 0.6 copy.21
